TPU v7x, 32 devices: a whole 2x2x4 slice. The times are simulated.
32 devices in a mesh: adapter: 8 (over z, x), feature: 4 (over y, core).
Axes of the slice: x: 2, y: 2, z: 4, core: 2. Of those that a mesh axis runs over, the one named last changes fastest.
Arguments:
- adapter_down: bfloat16 [128, 16, 8192], P('adapter', None, 'feature'), may hold values from -6 to 6
- adapter_up: bfloat16 [128, 16, 8192], P('adapter', None, 'feature'), may hold values from -6 to 6
- fisher: float32 [128], P('adapter'), may hold values from 0.1 to 10
- init_v: float32 [8192, 64], P('feature'), may hold values from -0.0625 to 0.0625
- init_u: float32 [8192, 64], P('feature'), may hold values from -0.0625 to 0.0625
- prompt_rows: bfloat16 [4096, 8192], P('adapter', 'feature'), may hold values from -6 to 6
- request_ids: int32 [32], P('adapter'), may hold values from 0 to 127
Outputs:
- served: bfloat16 [4096, 8192], P('adapter', 'feature')
All inputs are finite; a program needn't handle non-finite values.
Results may differ from a plain program's by a relative error of at most 0.025.
Values may be sent and summed in bfloat16 or wider, within the bound.
A program may use at most 64 MiB of HBM per device.

v0:
```python
import jax
import jax.numpy as jnp
from jax import lax
from jax.sharding import PartitionSpec as P

SWEEPS = 3


highest = lax.Precision.HIGHEST


def project(adapter_stack, basis_low):
    flat = adapter_stack.reshape(-1, adapter_stack.shape[-1])
    result = jnp.dot(flat, basis_low, preferred_element_type=jnp.float32)
    return result.reshape(adapter_stack.shape[0], adapter_stack.shape[1], -1)


def core_of(cols_q, rows_p):
    return jnp.einsum("irk,irl->ikl", cols_q, rows_p, precision=highest)


def numerator(adapter_stack, weighted):
    flat = adapter_stack.reshape(-1, adapter_stack.shape[-1])
    terms = weighted.reshape(-1, weighted.shape[-1])
    return lax.dot_general(
        flat, terms, (((0,), (0,)), ((), ())), preferred_element_type=jnp.float32
    )


def solve_with(gram_sum, matrix):
    factor = jnp.linalg.cholesky(gram_sum)
    return lax.linalg.triangular_solve(
        factor, matrix, left_side=False, lower=True, transpose_a=True
    )


def renew(local_term):
    full_term = lax.psum(local_term, "adapter")
    gram_sum = lax.psum(jnp.dot(full_term.T, full_term, precision=highest), "feature")
    return solve_with(gram_sum, full_term)


def down_sum(adapter_down, basis_v):
    return lax.psum(project(adapter_down, basis_v.astype(jnp.bfloat16)), "feature")


def up_sum(adapter_up, basis_u):
    return lax.psum(project(adapter_up, basis_u.astype(jnp.bfloat16)), "feature")


def on_device(adapter_down, adapter_up, fisher, init_v, init_u, prompt_rows, request_ids):
    basis_v = init_v
    basis_u = init_u
    weights = fisher[:, None, None]
    cols_q = up_sum(adapter_up, basis_u)
    for sweep_index in range(SWEEPS):
        rows_p = down_sum(adapter_down, basis_v)
        core_stack = core_of(cols_q, rows_p)
        weighted = (
            weights * jnp.einsum("irl,ikl->irk", rows_p, core_stack, precision=highest)
        ).astype(jnp.bfloat16)
        basis_u = renew(numerator(adapter_up, weighted))
        cols_q = up_sum(adapter_up, basis_u)
        core_stack = core_of(cols_q, rows_p)
        weighted = (
            weights * jnp.einsum("irk,ikl->irl", cols_q, core_stack, precision=highest)
        ).astype(jnp.bfloat16)
        basis_v = renew(numerator(adapter_down, weighted))
    rows_p = down_sum(adapter_down, basis_v)
    final_cores = core_of(cols_q, rows_p).astype(jnp.bfloat16)
    count_local = final_cores.shape[0]
    basis_width = final_cores.shape[1]
    flat_cores = final_cores.reshape(count_local, basis_width * basis_width)
    every_core = lax.all_gather(flat_cores, "adapter", axis=0, tiled=True)
    onehot = (
        request_ids[:, None] == jnp.arange(every_core.shape[0], dtype=jnp.int32)[None, :]
    ).astype(jnp.bfloat16)
    own_cores = jnp.dot(onehot, every_core, preferred_element_type=jnp.float32).astype(jnp.bfloat16)
    partial_rows = jnp.dot(
        prompt_rows, basis_v.astype(jnp.bfloat16), preferred_element_type=jnp.float32
    )
    hidden = lax.psum(partial_rows, "feature").astype(jnp.bfloat16)
    blocks = own_cores.shape[0]
    blocked = hidden.reshape(blocks, -1, basis_width)
    mixed_rows = jnp.einsum(
        "bnl,bkl->bnk",
        blocked,
        own_cores.reshape(blocks, basis_width, basis_width),
        preferred_element_type=jnp.float32,
    ).astype(jnp.bfloat16)
    served = jnp.dot(
        mixed_rows.reshape(-1, basis_width),
        basis_u.astype(jnp.bfloat16).T,
        preferred_element_type=jnp.float32,
    )
    return served.astype(jnp.bfloat16)


def solution(mesh):
    placed = (
        P("adapter", None, "feature"),
        P("adapter", None, "feature"),
        P("adapter"),
        P("feature", None),
        P("feature", None),
        P("adapter", "feature"),
        P("adapter"),
    )
    return jax.shard_map(
        on_device, mesh=mesh, in_specs=placed, out_specs=P("adapter", "feature"), check_vma=False
    )
```

profile of v0, /device:TPU:0, one launch (start us, length us, event | category | flops | bytes accessed | tf_op | source)
XLA Modules:
  0.0 935.1 jit_solution(6961525895619962585)
XLA Ops:
  6.5 2.6 fusion.15
  9.1 2.1 fusion.13
  11.3 35.2 %all-reduce.40.cloned.1.call-done = (f32[16,16,64]{2,1,0:T(8,128)}, f32[16,16,64]{2,1,0:T(8,128)}) async-done(((f32[16,16,64]{2,1,0:T(8,128)}, f32[16,16,64]{2,1,0:T(8,128)}), (f32[16,16,64]{2,1,0:T(8,128)}, f32[16,16,64]{2,1,0:T(8,128)})) %all-reduce.40.cloned.1.call-update) | async-done | bytes 131088 | tf_op jit(solution)/shard_map/psum | solution.py:44
  46.5 2.0 fusion.52
  48.5 1.8 fusion.6
  51.5 72.8 %all-reduce.16.cloned.1.call-done = f32[2048,64]{0,1:T(8,128)} async-done(((f32[2048,64]{0,1:T(8,128)}), f32[2048,64]{0,1:T(8,128)}) %all-reduce.16.cloned.1.call-update) | async-done | bytes 524304 | tf_op jit(solution)/shard_map/psum | solution.py:38
  124.3 1.8 fusion.53
  126.1 10.3 %psum.150 = f32[64,64]{0,1:T(8,128)S(1)} all-reduce(f32[64,64]{0,1:T(8,128)S(1)} %fusion.53), channel_id=1, replica_groups=mesh['adapter'=8,'feature'=4] {'feature'}, use_global_device_ids=true, to_apply=%region_3.0 | all-reduce | flops 4096 | bytes 32768 | tf_op jit(solution)/shard_map/psum | solution.py:39
  136.4 5.8 cholesky.104
  143.6 4.9 custom-call.10
  148.5 1.7 fusion
  151.5 31.2 %all-reduce.18.cloned.1.call-done = f32[16,16,64]{2,1,0:T(8,128)} async-done(((f32[16,16,64]{2,1,0:T(8,128)}), f32[16,16,64]{2,1,0:T(8,128)}) %all-reduce.18.cloned.1.call-update) | async-done | bytes 65552 | tf_op jit(solution)/shard_map/psum | solution.py:48
  182.7 1.9 fusion.54
  186.1 2.3 convolution_bitcast_fusion.10
  188.5 72.9 %all-reduce.20.cloned.1.call-done = f32[2048,64]{0,1:T(8,128)} async-done(((f32[2048,64]{0,1:T(8,128)}), f32[2048,64]{0,1:T(8,128)}) %all-reduce.20.cloned.1.call-update) | async-done | bytes 524304 | tf_op jit(solution)/shard_map/psum | solution.py:38
  261.4 1.8 fusion.55
  263.2 10.3 %psum.153 = f32[64,64]{0,1:T(8,128)S(1)} all-reduce(f32[64,64]{0,1:T(8,128)S(1)} %fusion.55), channel_id=1, replica_groups=mesh['adapter'=8,'feature'=4] {'feature'}, use_global_device_ids=true, to_apply=%region_8.11 | all-reduce | flops 4096 | bytes 32768 | tf_op jit(solution)/shard_map/psum | solution.py:39
  273.5 5.8 cholesky.115
  280.7 4.9 custom-call.11
  285.6 1.7 fusion.1
  287.3 1.7 convolution_bitcast_fusion.17
  290.0 31.1 %all-reduce.22.cloned.1.call-done = f32[16,16,64]{2,1,0:T(8,128)} async-done(((f32[16,16,64]{2,1,0:T(8,128)}), f32[16,16,64]{2,1,0:T(8,128)}) %all-reduce.22.cloned.1.call-update) | async-done | bytes 65552 | tf_op jit(solution)/shard_map/psum | solution.py:44
  321.0 1.9 fusion.56
  323.0 1.8 fusion.8
  326.0 72.9 %all-reduce.24.cloned.1.call-done = f32[2048,64]{0,1:T(8,128)} async-done(((f32[2048,64]{0,1:T(8,128)}), f32[2048,64]{0,1:T(8,128)}) %all-reduce.24.cloned.1.call-update) | async-done | bytes 524304 | tf_op jit(solution)/shard_map/psum | solution.py:38
  398.9 1.8 fusion.57
  400.7 10.3 %psum.156 = f32[64,64]{0,1:T(8,128)S(1)} all-reduce(f32[64,64]{0,1:T(8,128)S(1)} %fusion.57), channel_id=1, replica_groups=mesh['adapter'=8,'feature'=4] {'feature'}, use_global_device_ids=true, to_apply=%region_11.14 | all-reduce | flops 4096 | bytes 32768 | tf_op jit(solution)/shard_map/psum | solution.py:39
  411.0 5.8 cholesky.126
  418.2 4.9 custom-call.12
  423.1 1.7 fusion.2
  426.1 31.2 %all-reduce.26.cloned.1.call-done = f32[16,16,64]{2,1,0:T(8,128)} async-done(((f32[16,16,64]{2,1,0:T(8,128)}), f32[16,16,64]{2,1,0:T(8,128)}) %all-reduce.26.cloned.1.call-update) | async-done | bytes 65552 | tf_op jit(solution)/shard_map/psum | solution.py:48
  457.3 1.9 fusion.58
  460.7 2.3 convolution_bitcast_fusion.8
  463.1 72.9 %all-reduce.28.cloned.1.call-done = f32[2048,64]{0,1:T(8,128)} async-done(((f32[2048,64]{0,1:T(8,128)}), f32[2048,64]{0,1:T(8,128)}) %all-reduce.28.cloned.1.call-update) | async-done | bytes 524304 | tf_op jit(solution)/shard_map/psum | solution.py:38
  536.0 1.8 fusion.59
  537.8 10.3 %psum.159 = f32[64,64]{0,1:T(8,128)S(1)} all-reduce(f32[64,64]{0,1:T(8,128)S(1)} %fusion.59), channel_id=1, replica_groups=mesh['adapter'=8,'feature'=4] {'feature'}, use_global_device_ids=true, to_apply=%region_14.17 | all-reduce | flops 4096 | bytes 32768 | tf_op jit(solution)/shard_map/psum | solution.py:39
  548.1 5.8 cholesky.137
  555.3 4.9 custom-call.13
  560.2 1.7 fusion.3
  564.4 31.2 %all-reduce.30.cloned.1.call-done = f32[16,16,64]{2,1,0:T(8,128)} async-done(((f32[16,16,64]{2,1,0:T(8,128)}), f32[16,16,64]{2,1,0:T(8,128)}) %all-reduce.30.cloned.1.call-update) | async-done | bytes 65552 | tf_op jit(solution)/shard_map/psum | solution.py:44
  595.6 1.9 fusion.60
  597.5 1.8 fusion.10
  600.8 72.7 %all-reduce.32.cloned.1.call-done = f32[2048,64]{0,1:T(8,128)} async-done(((f32[2048,64]{0,1:T(8,128)}), f32[2048,64]{0,1:T(8,128)}) %all-reduce.32.cloned.1.call-update) | async-done | bytes 524304 | tf_op jit(solution)/shard_map/psum | solution.py:38
  673.5 1.8 fusion.61
  675.2 10.3 %psum.162 = f32[64,64]{0,1:T(8,128)S(1)} all-reduce(f32[64,64]{0,1:T(8,128)S(1)} %fusion.61), channel_id=1, replica_groups=mesh['adapter'=8,'feature'=4] {'feature'}, use_global_device_ids=true, to_apply=%region_17.20 | all-reduce | flops 4096 | bytes 32768 | tf_op jit(solution)/shard_map/psum | solution.py:39
  685.6 5.8 cholesky.148
  692.8 5.5 custom-call.14
  698.3 1.7 fusion.4
  701.1 1.7 copy.37
  702.8 31.2 %all-reduce.34.cloned.1.call-done = f32[16,16,64]{2,1,0:T(8,128)} async-done(((f32[16,16,64]{2,1,0:T(8,128)}), f32[16,16,64]{2,1,0:T(8,128)}) %all-reduce.34.cloned.1.call-update) | async-done | bytes 65552 | tf_op jit(solution)/shard_map/psum | solution.py:48
  734.1 1.9 fusion.62
  738.7 72.7 %all-reduce.36.cloned.1.call-done = f32[2048,64]{0,1:T(8,128)} async-done(((f32[2048,64]{0,1:T(8,128)}), f32[2048,64]{0,1:T(8,128)}) %all-reduce.36.cloned.1.call-update) | async-done | bytes 524304 | tf_op jit(solution)/shard_map/psum | solution.py:38
  811.4 2.4 fusion.63
  813.8 11.4 %psum.165 = f32[64,64]{0,1:T(8,128)} all-reduce(f32[64,64]{0,1:T(8,128)} %fusion.63), channel_id=1, replica_groups=mesh['adapter'=8,'feature'=4] {'feature'}, use_global_device_ids=true, to_apply=%region_20.23 | all-reduce | flops 4096 | bytes 32768 | tf_op jit(solution)/shard_map/psum | solution.py:39
  828.0 7.2 cholesky.159
  836.7 2.0 fusion.28
  838.7 6.3 custom-call.15
  845.0 1.7 fusion.5
  850.1 31.3 %all-reduce.38.cloned.1.call-done = f32[16,16,64]{2,1,0:T(8,128)} async-done(((f32[16,16,64]{2,1,0:T(8,128)}), f32[16,16,64]{2,1,0:T(8,128)}) %all-reduce.38.cloned.1.call-update) | async-done | bytes 65552 | tf_op jit(solution)/shard_map/psum | solution.py:44
  881.4 1.9 convolution_convert_fusion.2
  884.3 1.7 convolution_bitcast_fusion.12
  886.0 11.7 %all-reduce.41 = bf16[512,64]{0,1:T(8,128)(2,1)S(1)} all-reduce(f32[512,64]{0,1:T(8,128)S(1)} %convolution_bitcast_fusion.12), channel_id=1, replica_groups=mesh['adapter'=8,'feature'=4] {'feature'}, use_global_device_ids=true, to_apply=%region_21.24 | all-reduce | flops 32768 | bytes 196608 | tf_op jit(solution)/shard_map/psum | solution.py:82
  897.7 27.0 %all-gather.2.cloned.1.call-done = bf16[128,4096]{1,0:T(8,128)(2,1)} async-done(((bf16[16,4096]{1,0:T(8,128)(2,1)}), bf16[128,4096]{1,0:T(8,128)(2,1)}) %all-gather.2.cloned.1.call-update) | async-done | bytes 1048592 | tf_op jit(solution)/shard_map/all_gather | solution.py:74
  926.5 2.0 convolution_convert_fusion.1
  (102 shorter events, 34.2 us)
Async XLA Ops:
  6.5 877.8 %copy-start = (bf16[512,2048]{1,0:T(8,128)(2,1)S(1)}, bf16[512,2048]{1,0:T(8,128)(2,1)}, u32[]{:S(2)}) copy-start(bf16[512,2048]{1,0:T(8,128)(2,1)} %param.15) | copy-start | bytes 6291460
  6.5 2.6 copy-start.1
  6.5 41.9 %copy-start.10 = (f32[16]{0:T(128)S(1)}, f32[16]{0:T(128)}, u32[]{:S(2)}) copy-start(f32[16]{0:T(128)} %param.12) | copy-start | bytes 196
  6.5 40.0 %all-reduce.40.cloned.1.call-start = ((), (), s32[]{:S(2)}) async-start(), calls=%async_computation.13 | async-start | bytes 524288 | tf_op jit(solution)/shard_map/psum | solution.py:44
  11.3 113.0 %all-reduce.16.cloned.1.call-start = ((), (), s32[]{:S(2)}) async-start(), calls=%async_computation | async-start | bytes 1048576 | tf_op jit(solution)/shard_map/psum | solution.py:38
  51.5 131.2 %copy-start.4 = (f32[16,16,64]{2,1,0:T(8,128)S(1)}, f32[16,16,64]{2,1,0:T(8,128)}, u32[]{:S(2)}) copy-start(f32[16,16,64]{2,1,0:T(8,128)} %get-tuple-element.6) | copy-start | bytes 196612
  51.5 131.2 %all-reduce.18.cloned.1.call-start = ((), (), s32[]{:S(2)}) async-start(), calls=%async_computation.1 | async-start | bytes 262144 | tf_op jit(solution)/shard_map/psum | solution.py:48
  151.4 110.0 %all-reduce.20.cloned.1.call-start = ((), (), s32[]{:S(2)}) async-start(), calls=%async_computation.2 | async-start | bytes 1048576 | tf_op jit(solution)/shard_map/psum | solution.py:38
  188.5 132.6 %copy-start.5 = (f32[16,16,64]{2,1,0:T(8,128)S(1)}, f32[16,16,64]{2,1,0:T(8,128)}, u32[]{:S(2)}) copy-start(f32[16,16,64]{2,1,0:T(8,128)} %all-reduce.18.cloned.1.call-done) | copy-start | bytes 196612
  188.5 132.6 %all-reduce.22.cloned.1.call-start = ((), (), s32[]{:S(2)}) async-start(), calls=%async_computation.3 | async-start | bytes 262144 | tf_op jit(solution)/shard_map/psum | solution.py:44
  289.8 109.1 %all-reduce.24.cloned.1.call-start = ((), (), s32[]{:S(2)}) async-start(), calls=%async_computation.4 | async-start | bytes 1048576 | tf_op jit(solution)/shard_map/psum | solution.py:38
  325.9 131.4 %copy-start.6 = (f32[16,16,64]{2,1,0:T(8,128)S(1)}, f32[16,16,64]{2,1,0:T(8,128)}, u32[]{:S(2)}) copy-start(f32[16,16,64]{2,1,0:T(8,128)} %all-reduce.22.cloned.1.call-done) | copy-start | bytes 196612
  325.9 131.3 %all-reduce.26.cloned.1.call-start = ((), (), s32[]{:S(2)}) async-start(), calls=%async_computation.5 | async-start | bytes 262144 | tf_op jit(solution)/shard_map/psum | solution.py:48
  426.0 110.0 %all-reduce.28.cloned.1.call-start = ((), (), s32[]{:S(2)}) async-start(), calls=%async_computation.6 | async-start | bytes 1048576 | tf_op jit(solution)/shard_map/psum | solution.py:38
  463.1 132.6 %copy-start.7 = (f32[16,16,64]{2,1,0:T(8,128)S(1)}, f32[16,16,64]{2,1,0:T(8,128)}, u32[]{:S(2)}) copy-start(f32[16,16,64]{2,1,0:T(8,128)} %all-reduce.26.cloned.1.call-done) | copy-start | bytes 196612
  463.1 132.6 %all-reduce.30.cloned.1.call-start = ((), (), s32[]{:S(2)}) async-start(), calls=%async_computation.7 | async-start | bytes 262144 | tf_op jit(solution)/shard_map/psum | solution.py:44
  564.4 109.1 %all-reduce.32.cloned.1.call-start = ((), (), s32[]{:S(2)}) async-start(), calls=%async_computation.8 | async-start | bytes 1048576 | tf_op jit(solution)/shard_map/psum | solution.py:38
  600.5 133.5 %copy-start.8 = (f32[16,16,64]{2,1,0:T(8,128)S(1)}, f32[16,16,64]{2,1,0:T(8,128)}, u32[]{:S(2)}) copy-start(f32[16,16,64]{2,1,0:T(8,128)} %all-reduce.30.cloned.1.call-done) | copy-start | bytes 196612
  600.5 133.5 %all-reduce.34.cloned.1.call-start = ((), (), s32[]{:S(2)}) async-start(), calls=%async_computation.9 | async-start | bytes 262144 | tf_op jit(solution)/shard_map/psum | solution.py:48
  701.1 36.4 %copy-start.2 = (bf16[16,16,2048]{2,1,0:T(8,128)(2,1)S(1)}, bf16[16,16,2048]{2,1,0:T(8,128)(2,1)}, u32[]{:S(2)}) copy-start(bf16[16,16,2048]{2,1,0:T(8,128)(2,1)} %param.10) | copy-start | bytes 3145732
  702.8 108.6 %all-reduce.36.cloned.1.call-start = ((), (), s32[]{:S(2)}) async-start(), calls=%async_computation.10 | async-start | bytes 1048576 | tf_op jit(solution)/shard_map/psum | solution.py:38
  738.6 142.8 %copy-start.9 = (f32[16,16,64]{2,1,0:T(8,128)S(1)}, f32[16,16,64]{2,1,0:T(8,128)}, u32[]{:S(2)}) copy-start(f32[16,16,64]{2,1,0:T(8,128)} %all-reduce.34.cloned.1.call-done) | copy-start | bytes 196612
  738.6 142.8 %all-reduce.38.cloned.1.call-start = ((), (), s32[]{:S(2)}) async-start(), calls=%async_computation.11 | async-start | bytes 262144 | tf_op jit(solution)/shard_map/psum | solution.py:44
  846.6 0.7 copy-start.3
  848.4 76.3 %copy-start.11 = (s32[4]{0:T(128)S(1)}, s32[4]{0:T(128)}, u32[]{:S(2)}) copy-start(s32[4]{0:T(128)} %param.16) | copy-start | bytes 52
  850.0 74.7 %all-gather.2.cloned.1.call-start = ((), (), s32[]{:S(2)}) async-start(), calls=%async_computation.12 | async-start | bytes 1179648 | tf_op jit(solution)/shard_map/all_gather | solution.py:74
Sparse Core Ops, SparseCore 0:
  11.4 35.0 all-reduce.39
  51.6 72.6 all-reduce.15
  151.5 31.1 all-reduce.17
  188.6 72.7 all-reduce.19
  289.9 31.1 all-reduce.21
  326.1 72.7 all-reduce.23
  426.1 31.1 all-reduce.25
  463.2 72.7 all-reduce.27
  564.5 31.1 all-reduce.29
  600.6 72.7 all-reduce.31
  702.9 31.1 all-reduce.33
  738.7 72.6 all-reduce.35
  850.2 31.2 all-reduce.37
  884.4 40.2 all-gather.1
where the time goes:
time: 937 us; the launch traced here: 935 us
  waiting for transfers between devices  686 us (73%)
  other arithmetic  79.4 us (8%)
  blocking collectives  74.4 us (8%)
  matrix products  70.3 us (8%)
  between operations  13.7 us (1%)
  local copies, waits for them, and re-layouts  9.93 us (1%)
    psum x6, waiting for transfers between devices, renew(): full_term = lax.psum(local_term, 'adapter')  437 us
    psum x4, waiting for transfers between devices, down_sum(): lax.psum(project(adapter_down, basis_v.astype(jnp.bfloat16)), 'feature')  129 us
    psum x3, waiting for transfers between devices, up_sum(): lax.psum(project(adapter_up, basis_u.astype(jnp.bfloat16)), 'feature')  93.7 us
    psum x6, blocking collectives, renew(): lax.psum(jnp.dot(full_term.T, full_term, precision=highest), 'feature')  62.7 us
    another operation x18, other arithmetic, solve_with(): factor = jnp.linalg.cholesky(gram_sum)  41.3 us
    another operation x12, other arithmetic, solve_with(): lax.linalg.triangular_solve(factor, matrix, left_side=False, lower=True,...  36.7 us
    all_gather x1, waiting for transfers between devices, on_device(): every_core = lax.all_gather(flat_cores, 'adapter', axis=0, tiled=True)  27 us
  transfers between devices with their start and end apart: 14, of which 14 were waited for; matrix products, arithmetic and copies ran while one was open for 0% of the time, Pallas kernels for 0%

commit v1 on v0

v1 whole, which is shorter than its diff:
```python
import functools

import jax
import jax.numpy as jnp
from jax import lax
from jax.experimental import pallas as pl
from jax.experimental.pallas import tpu as pltpu
from jax.sharding import PartitionSpec as P

SWEEPS = 3
GROUP = 8


highest = lax.Precision.HIGHEST


def dot32(left, right):
    return jnp.dot(left, right, precision=highest, preferred_element_type=jnp.float32)


def dot_nt(left, right):
    return lax.dot_general(
        left, right, (((1,), (1,)), ((), ())), preferred_element_type=jnp.float32
    )


def inverse_factor(gram):
    width = gram.shape[0]
    rows = lax.broadcasted_iota(jnp.int32, (width, width), 0)
    columns = lax.broadcasted_iota(jnp.int32, (width, width), 1)
    eye = (rows == columns).astype(jnp.float32)
    table = jnp.concatenate([gram, eye], axis=1)
    blocks = [table[at : at + GROUP] for at in range(0, width, GROUP)]
    inner = lax.broadcasted_iota(jnp.int32, (GROUP, 1), 0)
    for k in range(width):
        first, offset = divmod(k, GROUP)
        row = blocks[first][offset : offset + 1]
        scaled = row / row[:, k : k + 1]
        for b in range(first, len(blocks)):
            factor = blocks[b][:, k : k + 1]
            if b == first:
                factor = jnp.where(inner > offset, factor, 0.0)
            blocks[b] = blocks[b] - factor * scaled
    table = jnp.concatenate(blocks, axis=0)
    pivots = jnp.sum(table[:, :width] * eye, axis=1, keepdims=True)
    return table[:, width:] / jnp.sqrt(pivots)


def weigh(rank, fresh, other, weights):
    total = fresh.shape[1]
    step = 128 if total % 128 == 0 and 128 % rank == 0 else total
    same = (
        lax.broadcasted_iota(jnp.int32, (step, step), 0) // rank
        == lax.broadcasted_iota(jnp.int32, (step, step), 1) // rank
    )
    parts = []
    for at in range(0, total, step):
        piece = fresh[:, at : at + step]
        inner = jnp.where(same, dot32(piece.T, piece), 0.0)
        parts.append(dot32(other[:, at : at + step], inner))
    joined = parts[0] if len(parts) == 1 else jnp.concatenate(parts, axis=1)
    return (joined * weights).astype(jnp.bfloat16)


def first_kernel(rank, fresh_ref, other_ref, weights_ref, flat_ref, term_ref):
    low = weigh(rank, fresh_ref[...], other_ref[...], weights_ref[...])
    term_ref[...] = jnp.dot(low, flat_ref[...], preferred_element_type=jnp.float32)


def turn_kernel(rank, sums_ref, other_ref, weights_ref, flat_ref, inverse_ref, fresh_ref, term_ref):
    extent = fresh_ref.shape[1]
    inverse = inverse_factor(sums_ref[:, extent:])
    inverse_ref[...] = inverse
    fresh = dot32(inverse, sums_ref[:, :extent])
    fresh_ref[...] = fresh
    low = weigh(rank, fresh, other_ref[...], weights_ref[...])
    term_ref[...] = jnp.dot(low, flat_ref[...], preferred_element_type=jnp.float32)


def last_kernel(sums_ref, fresh_ref):
    extent = fresh_ref.shape[1]
    inverse = inverse_factor(sums_ref[:, extent:])
    fresh_ref[...] = dot32(inverse, sums_ref[:, :extent])


def gram_kernel(full_ref, *refs):
    full = full_ref[...]
    high = full.astype(jnp.bfloat16)
    low = (full - high.astype(jnp.float32)).astype(jnp.bfloat16)
    both = jnp.concatenate([high, low], axis=0)
    width = full.shape[0]
    *stacks, sums_ref = refs
    at = 0
    for stack in stacks:
        pair = dot_nt(both, stack[...])
        sums_ref[:, at : at + pair.shape[1]] = pair[:width] + pair[width:]
        at += pair.shape[1]
    quad = dot_nt(both, both)
    half = quad[:width] + quad[width:]
    sums_ref[:, at : at + width] = half[:, :width] + half[:, width:]


def call(body, shapes, *args):
    return pl.pallas_call(
        body,
        out_shape=[jax.ShapeDtypeStruct(shape, jnp.float32) for shape in shapes],
        compiler_params=pltpu.CompilerParams(vmem_limit_bytes=40 * 2**20),
    )(*args)


def on_device(adapter_down, adapter_up, fisher, init_v, init_u, prompt_rows, request_ids):
    count_local, rank, depth = adapter_up.shape
    width = init_v.shape[1]
    rows = count_local * rank
    down = adapter_down.reshape(rows, depth)
    up = adapter_up.reshape(rows, depth)
    weights = jnp.repeat(fisher, rank)[None, :]

    def start(basis, flat):
        return lax.dot_general(
            basis.astype(jnp.bfloat16),
            flat,
            (((0,), (1,)), ((), ())),
            preferred_element_type=jnp.float32,
        )

    def sums(full, *stacks):
        extent = sum(stack.shape[0] for stack in stacks)
        (partial,) = call(gram_kernel, [(width, extent + width)], full, *stacks)
        return lax.psum(partial, "feature")

    both = lax.psum(
        jnp.concatenate([start(init_v, down), start(init_u, up)], axis=1), "feature"
    )
    rows_p, cols_q = both[:, :rows], both[:, rows:]
    shape_term, shape_rows, shape_gram = (width, depth), (width, rows), (width, width)
    (term,) = call(
        functools.partial(first_kernel, rank), [shape_term], rows_p, cols_q, weights, up
    )
    turn = functools.partial(turn_kernel, rank)
    shapes = [shape_gram, shape_rows, shape_term]
    for sweep_index in range(SWEEPS):
        full_u = lax.psum(term, "adapter")
        total = sums(full_u, up)
        inverse_u, cols_q, term = call(turn, shapes, total, rows_p, weights, down)
        full_v = lax.psum(term, "adapter")
        if sweep_index < SWEEPS - 1:
            total = sums(full_v, down)
            _, rows_p, term = call(turn, shapes, total, cols_q, weights, up)
    total = sums(full_v, down, prompt_rows)
    (fresh,) = call(last_kernel, [(width, rows + prompt_rows.shape[0])], total)
    rows_p, hidden = fresh[:, :rows], fresh[:, rows:].astype(jnp.bfloat16)
    basis_u = dot32(inverse_u, full_u).astype(jnp.bfloat16)
    final_cores = jnp.einsum(
        "kir,lir->ikl",
        cols_q.reshape(width, count_local, rank),
        rows_p.reshape(width, count_local, rank),
        precision=highest,
    ).astype(jnp.bfloat16)
    flat_cores = final_cores.reshape(count_local, width * width)
    every_core = lax.all_gather(flat_cores, "adapter", axis=0, tiled=True)
    onehot = (
        request_ids[:, None] == jnp.arange(every_core.shape[0], dtype=jnp.int32)[None, :]
    ).astype(jnp.bfloat16)
    own_cores = jnp.dot(onehot, every_core, preferred_element_type=jnp.float32).astype(jnp.bfloat16)
    blocks = own_cores.shape[0]
    mixed = jnp.einsum(
        "lbn,bkl->bnk",
        hidden.reshape(width, blocks, -1),
        own_cores.reshape(blocks, width, width),
        preferred_element_type=jnp.float32,
    ).astype(jnp.bfloat16)
    served = jnp.dot(
        mixed.reshape(-1, width), basis_u, preferred_element_type=jnp.float32
    )
    return served.astype(jnp.bfloat16)


def solution(mesh):
    placed = (
        P("adapter", None, "feature"),
        P("adapter", None, "feature"),
        P("adapter"),
        P("feature", None),
        P("feature", None),
        P("adapter", "feature"),
        P("adapter"),
    )
    return jax.shard_map(
        on_device, mesh=mesh, in_specs=placed, out_specs=P("adapter", "feature"), check_vma=False
    )
```

time: 937 us -> 791 us (0.84)
  other arithmetic: 79.4 us -> 0.67 us
  blocking collectives: 74.4 us -> 0 us
  matrix products: 70.3 us -> 9.07 us
  Pallas kernels: 0 us -> 53.1 us
  waiting for transfers between devices: 686 us -> 698 us
    another operation x30 -> x0, other arithmetic: 77.9 us -> none  [the longest x18 41.3 us: solve_with(): factor = jnp.linalg.cholesky(gram_sum)]
    psum x7 -> x0, blocking collectives: 74.4 us -> none  [the longest x6 62.7 us: renew(): lax.psum(jnp.dot(full_term.T, full_term, precision=highest), 'feature')]
    pallas_call x0 -> x13, Pallas kernels: none -> 53.1 us  [call(): pl.pallas_call(body, out_shape=[jax.ShapeDtypeStruct(shape, jnp.float32)...]
    dot_general x36 -> x6, matrix products: 58.7 us -> 7.55 us  [the longest x2 3.76 us: start(): lax.dot_general(basis.astype(jnp.bfloat16), flat, (((0,), (1,)), ((), ())...]
    all_gather x1, waiting for transfers between devices: 27 us -> 39.8 us  [on_device(): every_core = lax.all_gather(flat_cores, 'adapter', axis=0, tiled=True)]
    unnamed x24 -> x36, local copies, waits for them, and re-layouts: 0.74 us -> 13.3 us
    another operation x6 -> x0, matrix products: 10.1 us -> none  [solve_with(): lax.linalg.triangular_solve(factor, matrix, left_side=False, lower=True,...]
where the time goes in v1:
time: 791 us; the launch traced here: 790 us
  waiting for transfers between devices  698 us (88%)
  Pallas kernels  53.1 us (7%)
  local copies, waits for them, and re-layouts  15.5 us (2%)
  between operations  13.4 us (2%)
  matrix products  9.07 us (1%)
    psum x3, waiting for transfers between devices, on_device(): full_u = lax.psum(term, 'adapter')  219 us
    psum x3, waiting for transfers between devices, on_device(): full_v = lax.psum(term, 'adapter')  218 us
    psum x6, waiting for transfers between devices, sums(): return lax.psum(partial, 'feature')  186 us
    pallas_call x13, Pallas kernels, call(): pl.pallas_call(body, out_shape=[jax.ShapeDtypeStruct(shape, jnp.float32)...  53.1 us
    all_gather x1, waiting for transfers between devices, on_device(): every_core = lax.all_gather(flat_cores, 'adapter', axis=0, tiled=True)  39.8 us
    psum x1, waiting for transfers between devices, on_device(): lax.psum(jnp.concatenate([start(init_v, down), start(init_u, up)], axis=1...  34.5 us
  transfers between devices with their start and end apart: 14, of which 14 were waited for; matrix products, arithmetic and copies ran while one was open for 0% of the time, Pallas kernels for 0%

profile of v1, /device:TPU:0, one launch (start us, length us, event | category | flops | bytes accessed | tf_op | source)
XLA Modules:
  0.0 790.3 jit_solution(9633796602967134183)
XLA Ops:
  6.5 1.9 fusion.3
  8.5 1.8 fusion.1
  10.3 0.7 pad_maximum_fusion
  11.0 0.0 all-reduce.16.cloned.1.call-start
  11.1 0.1 broadcast_in_dim.2
  11.1 0.1 broadcast_in_dim_reshape.3.weights_ref
  11.2 34.5 %all-reduce.14.cloned.1.call-done = f32[64,512]{1,0:T(8,128)} async-done(((f32[64,512]{1,0:T(8,128)}), f32[64,512]{1,0:T(8,128)}) %all-reduce.14.cloned.1.call-update) | async-done | bytes 131088 | tf_op jit(solution)/shard_map/psum | solution.py:132
  45.7 0.9 fusion.11
  46.6 1.7 shard_map.73
  48.3 73.6 %all-reduce.16.cloned.1.call-done.full_ref = f32[64,2048]{1,0:T(8,128)} async-done(((f32[64,2048]{1,0:T(8,128)}), f32[64,2048]{1,0:T(8,128)}) %all-reduce.16.cloned.1.call-update) | async-done | bytes 524304 | tf_op jit(solution)/shard_map/psum | solution.py:143
  121.9 1.0 copy-done.5
  122.9 1.3 shard_map.74
  124.3 31.0 %all-reduce.18.cloned.1.call-done.sums_ref = f32[64,320]{1,0:T(8,128)} async-done(((f32[64,320]{1,0:T(8,128)}), f32[64,320]{1,0:T(8,128)}) %all-reduce.18.cloned.1.call-update) | async-done | bytes 81936 | tf_op jit(solution)/shard_map/psum | solution.py:130
  155.3 0.9 copy-done.15
  156.2 7.4 shard_map.75
  163.6 0.0 all-reduce.22.cloned.1.call-start
  163.7 72.8 %all-reduce.20.cloned.1.call-done.full_ref = f32[64,2048]{1,0:T(8,128)} async-done(((f32[64,2048]{1,0:T(8,128)}), f32[64,2048]{1,0:T(8,128)}) %all-reduce.20.cloned.1.call-update) | async-done | bytes 524304 | tf_op jit(solution)/shard_map/psum | solution.py:146
  236.4 1.0 copy-done.6
  237.5 1.3 shard_map.76
  238.8 0.0 all-reduce.24.cloned.1.call-start
  238.8 31.0 %all-reduce.22.cloned.1.call-done.sums_ref = f32[64,320]{1,0:T(8,128)} async-done(((f32[64,320]{1,0:T(8,128)}), f32[64,320]{1,0:T(8,128)}) %all-reduce.22.cloned.1.call-update) | async-done | bytes 81936 | tf_op jit(solution)/shard_map/psum | solution.py:130
  269.8 0.9 copy-done.12
  270.7 7.4 shard_map.77
  278.2 72.8 %all-reduce.24.cloned.1.call-done.full_ref = f32[64,2048]{1,0:T(8,128)} async-done(((f32[64,2048]{1,0:T(8,128)}), f32[64,2048]{1,0:T(8,128)}) %all-reduce.24.cloned.1.call-update) | async-done | bytes 524304 | tf_op jit(solution)/shard_map/psum | solution.py:143
  350.9 1.0 copy-done.7
  351.9 1.3 shard_map.78
  353.3 0.0 all-reduce.28.cloned.1.call-start
  353.3 31.0 %all-reduce.26.cloned.1.call-done.sums_ref = f32[64,320]{1,0:T(8,128)} async-done(((f32[64,320]{1,0:T(8,128)}), f32[64,320]{1,0:T(8,128)}) %all-reduce.26.cloned.1.call-update) | async-done | bytes 81936 | tf_op jit(solution)/shard_map/psum | solution.py:130
  384.3 0.9 copy-done.13
  385.2 7.4 shard_map.79
  392.7 72.8 %all-reduce.28.cloned.1.call-done.full_ref = f32[64,2048]{1,0:T(8,128)} async-done(((f32[64,2048]{1,0:T(8,128)}), f32[64,2048]{1,0:T(8,128)}) %all-reduce.28.cloned.1.call-update) | async-done | bytes 524304 | tf_op jit(solution)/shard_map/psum | solution.py:146
  465.4 1.0 copy-done.8
  466.5 1.3 shard_map.80
  467.8 0.0 all-reduce.32.cloned.1.call-start
  467.8 31.0 %all-reduce.30.cloned.1.call-done.sums_ref = f32[64,320]{1,0:T(8,128)} async-done(((f32[64,320]{1,0:T(8,128)}), f32[64,320]{1,0:T(8,128)}) %all-reduce.30.cloned.1.call-update) | async-done | bytes 81936 | tf_op jit(solution)/shard_map/psum | solution.py:130
  498.8 0.9 copy-done.14
  499.7 7.4 shard_map.81
  507.1 0.0 all-reduce.34.cloned.1.call-start
  507.2 72.8 %all-reduce.32.cloned.1.call-done.full_ref = f32[64,2048]{1,0:T(8,128)} async-done(((f32[64,2048]{1,0:T(8,128)}), f32[64,2048]{1,0:T(8,128)}) %all-reduce.32.cloned.1.call-update) | async-done | bytes 524304 | tf_op jit(solution)/shard_map/psum | solution.py:143
  579.9 1.0 copy-done.2
  581.0 1.3 shard_map.82
  582.3 0.2 all-reduce.36.cloned.1.call-start
  582.5 30.8 %all-reduce.34.cloned.1.call-done.sums_ref = f32[64,320]{1,0:T(8,128)} async-done(((f32[64,320]{1,0:T(8,128)}), f32[64,320]{1,0:T(8,128)}) %all-reduce.34.cloned.1.call-update) | async-done | bytes 81936 | tf_op jit(solution)/shard_map/psum | solution.py:130
  613.3 0.9 copy-done.11
  614.2 7.4 shard_map.83
  621.6 0.0 all-reduce.38.cloned.1.call-start
  621.7 72.7 %all-reduce.36.cloned.1.call-done.full_ref = f32[64,2048]{1,0:T(8,128)} async-done(((f32[64,2048]{1,0:T(8,128)}), f32[64,2048]{1,0:T(8,128)}) %all-reduce.36.cloned.1.call-update) | async-done | bytes 524304 | tf_op jit(solution)/shard_map/psum | solution.py:146
  694.4 1.6 copy-done.4
  696.0 1.0 copy-done.9
  697.1 2.0 shard_map.84
  699.1 0.0 all-gather.2.cloned.1.call-start
  699.2 0.1 copy.11
  699.3 31.4 %all-reduce.38.cloned.1.call-done.sums_ref = f32[64,832]{1,0:T(8,128)} async-done(((f32[64,832]{1,0:T(8,128)}), f32[64,832]{1,0:T(8,128)}) %all-reduce.38.cloned.1.call-update) | async-done | bytes 213008 | tf_op jit(solution)/shard_map/psum | solution.py:130
  730.6 0.9 copy-done.10
  731.6 5.8 shard_map.85
  737.4 0.1 copy.12
  737.5 1.0 convolution_convert_fusion.3
  738.5 0.9 reshape.30
  739.5 0.6 convolution_convert_fusion.2
  740.1 39.8 %all-gather.2.cloned.1.call-done = bf16[128,4096]{1,0:T(8,128)(2,1)} async-done(((bf16[16,4096]{1,0:T(8,128)(2,1)}), bf16[128,4096]{1,0:T(8,128)(2,1)}) %all-gather.2.cloned.1.call-update) | async-done | bytes 1048592 | tf_op jit(solution)/shard_map/all_gather | solution.py:161
  779.9 1.5 convolution_convert_fusion
  781.5 0.1 reshape.31
  781.6 0.1 fusion
  781.7 2.1 convolution_convert_fusion.1
  (43 shorter events, 0.4 us)
Async XLA Ops:
  6.5 40.0 %copy-start = (bf16[16,16,2048]{2,1,0:T(8,128)(2,1)S(1)}, bf16[16,16,2048]{2,1,0:T(8,128)(2,1)}, u32[]{:S(2)}) copy-start(bf16[16,16,2048]{2,1,0:T(8,128)(2,1)} %param.8) | copy-start | bytes 3145732
  6.5 4.5 copy-start.17
  6.5 39.1 %all-reduce.14.cloned.1.call-start = ((), (), s32[]{:S(2)}) async-start(), calls=%async_computation | async-start | bytes 262144 | tf_op jit(solution)/shard_map/psum | solution.py:132
  11.0 110.9 %all-reduce.16.cloned.1.call-start = ((), (), s32[]{:S(2)}) async-start(), calls=%async_computation.1 | async-start | bytes 1048576 | tf_op jit(solution)/shard_map/psum | solution.py:143
  11.2 144.1 %copy-start.1 = (bf16[16,16,2048]{2,1,0:T(8,128)(2,1)S(1)}, bf16[16,16,2048]{2,1,0:T(8,128)(2,1)}, u32[]{:S(2)}) copy-start(bf16[16,16,2048]{2,1,0:T(8,128)(2,1)} %param.7) | copy-start | bytes 3145732
  48.2 107.0 %all-reduce.18.cloned.1.call-start = ((), (), s32[]{:S(2)}) async-start(), calls=%async_computation.2 | async-start | bytes 196608 | tf_op jit(solution)/shard_map/psum | solution.py:130
  121.9 1.0 copy-start.5
  124.3 112.1 %all-reduce.20.cloned.1.call-start = ((), (), s32[]{:S(2)}) async-start(), calls=%async_computation.3 | async-start | bytes 1048576 | tf_op jit(solution)/shard_map/psum | solution.py:146
  155.3 0.9 copy-start.15
  163.6 106.2 %all-reduce.22.cloned.1.call-start = ((), (), s32[]{:S(2)}) async-start(), calls=%async_computation.4 | async-start | bytes 196608 | tf_op jit(solution)/shard_map/psum | solution.py:130
  236.4 1.0 copy-start.6
  238.8 112.1 %all-reduce.24.cloned.1.call-start = ((), (), s32[]{:S(2)}) async-start(), calls=%async_computation.5 | async-start | bytes 1048576 | tf_op jit(solution)/shard_map/psum | solution.py:143
  269.8 0.9 copy-start.12
  278.1 106.2 %all-reduce.26.cloned.1.call-start = ((), (), s32[]{:S(2)}) async-start(), calls=%async_computation.6 | async-start | bytes 196608 | tf_op jit(solution)/shard_map/psum | solution.py:130
  350.9 1.0 copy-start.7
  353.3 112.1 %all-reduce.28.cloned.1.call-start = ((), (), s32[]{:S(2)}) async-start(), calls=%async_computation.7 | async-start | bytes 1048576 | tf_op jit(solution)/shard_map/psum | solution.py:146
  384.3 0.9 copy-start.13
  392.6 106.2 %all-reduce.30.cloned.1.call-start = ((), (), s32[]{:S(2)}) async-start(), calls=%async_computation.8 | async-start | bytes 196608 | tf_op jit(solution)/shard_map/psum | solution.py:130
  465.4 1.0 copy-start.8
  467.8 112.1 %all-reduce.32.cloned.1.call-start = ((), (), s32[]{:S(2)}) async-start(), calls=%async_computation.9 | async-start | bytes 1048576 | tf_op jit(solution)/shard_map/psum | solution.py:143
  498.8 0.9 copy-start.14
  507.1 106.2 %all-reduce.34.cloned.1.call-start = ((), (), s32[]{:S(2)}) async-start(), calls=%async_computation.10 | async-start | bytes 196608 | tf_op jit(solution)/shard_map/psum | solution.py:130
  579.9 1.0 copy-start.2
  582.3 112.1 %all-reduce.36.cloned.1.call-start = ((), (), s32[]{:S(2)}) async-start(), calls=%async_computation.11 | async-start | bytes 1048576 | tf_op jit(solution)/shard_map/psum | solution.py:146
  613.3 0.9 copy-start.11
  621.6 117.9 %copy-start.3 = (f32[64,2048]{1,0:T(8,128)S(1)}, f32[64,2048]{1,0:T(8,128)}, u32[]{:S(2)}) copy-start(f32[64,2048]{1,0:T(8,128)} %all-reduce.32.cloned.1.call-done.full_ref) | copy-start | bytes 1572868
  621.6 109.0 %all-reduce.38.cloned.1.call-start = ((), (), s32[]{:S(2)}) async-start(), calls=%async_computation.12 | async-start | bytes 458752 | tf_op jit(solution)/shard_map/psum | solution.py:130
  694.4 1.6 copy-start.4
  696.0 1.0 copy-start.9
  699.1 80.8 %copy-start.16 = (s32[4]{0:T(128)S(1)}, s32[4]{0:T(128)}, u32[]{:S(2)}) copy-start(s32[4]{0:T(128)} %param.13) | copy-start | bytes 52
  699.1 80.8 %all-gather.2.cloned.1.call-start = ((), (), s32[]{:S(2)}) async-start(), calls=%async_computation.13 | async-start | bytes 1179648 | tf_op jit(solution)/shard_map/all_gather | solution.py:161
  730.6 0.9 copy-start.10
Sparse Core Ops, SparseCore 0:
  11.1 34.5 all-reduce.13
  49.1 72.7 all-reduce.15
  124.4 30.8 all-reduce.17
  163.7 72.6 all-reduce.19
  238.9 30.8 all-reduce.21
  278.2 72.6 all-reduce.23
  353.4 30.8 all-reduce.25
  392.7 72.6 all-reduce.27
  467.9 30.8 all-reduce.29
  507.2 72.6 all-reduce.31
  582.4 30.8 all-reduce.33
  621.7 72.6 all-reduce.35
  699.2 31.3 all-reduce.37
  739.6 40.2 all-gather.1
